TPU v7x, 32 devices: a whole 2x2x4 slice. The times are simulated.
32 devices in a mesh: dp: 8 (over y, x, core), mp: 4 (over z).
Axes of the slice: x: 2, y: 2, z: 4, core: 2. Of those that a mesh axis runs over, the one named last changes fastest.
Arguments:
- inputs: bfloat16 [8192, 2048], P('dp'), may hold values from -6 to 6
- segments: int32 [8192], P('dp'), may hold values from 0 to 511, as said below
- padding: int32 [8192], P('dp'), may hold values from 0 to 1, as said below
- first_gain: bfloat16 [2048], P('dp'), may hold values from 0.5 to 1.5
- first_shift: bfloat16 [2048], P('dp'), may hold values from -4 to 4
- second_gain: bfloat16 [2048], P('dp'), may hold values from 0.5 to 1.5
- second_shift: bfloat16 [2048], P('dp'), may hold values from -4 to 4
- joint_weight: bfloat16 [2048, 6144], P('dp', 'mp'), may hold values from -1 to 1
- joint_bias: bfloat16 [6144], P(('mp', 'dp')), may hold values from -4 to 4
- dense_weight: bfloat16 [2048, 2048], P('mp', 'dp'), may hold values from -0.75 to 0.75
- dense_bias: bfloat16 [2048], P('dp'), may hold values from -4 to 4
- expand_weight: bfloat16 [2048, 8192], P('dp', 'mp'), may hold values from -0.125 to 0.125
- expand_bias: bfloat16 [8192], P(('mp', 'dp')), may hold values from -6 to 6
- reduce_weight: bfloat16 [8192, 2048], P('mp', 'dp'), may hold values from -0.0625 to 0.0625
- reduce_bias: bfloat16 [2048], P('dp'), may hold values from -4 to 4
- cotangent: bfloat16 [8192, 2048], P('dp'), may hold values from -6 to 6
Outputs:
- result: bfloat16 [8192, 2048], P('dp')
- inputs_back: bfloat16 [8192, 2048], P('dp')
- first_gain_back: float32 [2048], P('dp')
- first_shift_back: float32 [2048], P('dp')
- second_gain_back: float32 [2048], P('dp')
- second_shift_back: float32 [2048], P('dp')
- joint_weight_back: float32 [2048, 6144], P('dp', 'mp')
- joint_bias_back: float32 [6144], P(('mp', 'dp'))
- dense_weight_back: float32 [2048, 2048], P('mp', 'dp')
- dense_bias_back: float32 [2048], P('dp')
- expand_weight_back: float32 [2048, 8192], P('dp', 'mp')
- expand_bias_back: float32 [8192], P(('mp', 'dp'))
- reduce_weight_back: float32 [8192, 2048], P('mp', 'dp')
- reduce_bias_back: float32 [2048], P('dp')
Inputs may be any that keep to these rules, and one draw needn't show every extreme that they name: `segments`: within each aligned block of 512 rows the ids never fall from row to row; a block ends with 1 to 384 padding rows that carry the id 512 - 1, and its sequences carry smaller ids; no sequence crosses a block's end. 0 exactly on the padding rows that end each block of 512 rows.
All inputs are finite; a program needn't handle non-finite values.
Results may differ from a plain program's by a relative error of at most 0.018.
Values may be sent and summed in bfloat16 or wider, within the bound.
No kernel may reach another device: no remote copies, remote signals or barrier semaphores. Data moves between devices by JAX's collectives and lax.ppermute only.
A program may use at most 256 MiB of HBM per device.

v0:
```python
import math
import jax
import jax.numpy as jnp
from jax import lax
from jax.sharding import PartitionSpec as P

HD = 256
ROT = 64
MICRO = 2
EPS = 1e-05
NEGATIVE = -1e30
ROOT_HALF = 0.7071067811865476
ROOT_TWOPI = 2.5066282746310002


def normalize(matrix):
    centred = matrix - jnp.mean(matrix, axis=1, keepdims=True)
    scale_inv = lax.rsqrt(jnp.mean(centred * centred, axis=1, keepdims=True) + EPS)
    return (centred * scale_inv, scale_inv)


def layout(labels):
    indices = jnp.arange(labels.shape[0])
    matching = labels[:, None] == labels[None, :]
    earlier = indices[None, :] < indices[:, None]
    positions = jnp.sum((matching & earlier).astype(jnp.int32), axis=1).astype(jnp.float32)
    allowed = matching & (indices[None, :] <= indices[:, None])
    return (positions, allowed)


def rotary_tables(positions):
    half_width = ROT // 2
    frequency = jnp.exp(
        jnp.arange(half_width, dtype=jnp.float32) * (-2.0 * math.log(10000.0) / ROT)
    )
    angles = positions[:, None] * frequency[None, :]
    return (jnp.cos(angles)[:, None, :], jnp.sin(angles)[:, None, :])


def rotate(tensor, cosine_table, sine_table):
    half_width = ROT // 2
    leading = tensor[..., :half_width]
    trailing = tensor[..., half_width:ROT]
    remain = tensor[..., ROT:]
    return jnp.concatenate(
        [
            leading * cosine_table - trailing * sine_table,
            trailing * cosine_table + leading * sine_table,
            remain,
        ],
        axis=-1,
    )


def unrotate(tensor, cosine_table, sine_table):
    half_width = ROT // 2
    leading = tensor[..., :half_width]
    trailing = tensor[..., half_width:ROT]
    remain = tensor[..., ROT:]
    return jnp.concatenate(
        [
            leading * cosine_table + trailing * sine_table,
            trailing * cosine_table - leading * sine_table,
            remain,
        ],
        axis=-1,
    )


def gelu_value(values):
    return 0.5 * values * (1.0 + lax.erf(values * ROOT_HALF))


def gelu_slope(values):
    return (
        0.5 * (1.0 + lax.erf(values * ROOT_HALF))
        + values * jnp.exp(-0.5 * values * values) / ROOT_TWOPI
    )


def attend_forward(queries, key_rows, value_rows, allowed):
    total_rows, head_count, head_depth = queries.shape
    block_rows = min(512, total_rows)
    block_count = total_rows // block_rows

    def one_block(pieces):
        query_block, mask_block = pieces
        scores = jnp.einsum(
            "qhd,khd->hqk", query_block, key_rows, preferred_element_type=jnp.float32
        )
        scores = jnp.where(mask_block[None], scores, NEGATIVE)
        row_peak = jnp.max(scores, axis=2, keepdims=True)
        logsum = row_peak + jnp.log(jnp.sum(jnp.exp(scores - row_peak), axis=2, keepdims=True))
        weights = jnp.exp(scores - logsum).astype(jnp.bfloat16)
        mixture = jnp.einsum(
            "hqk,khd->qhd", weights, value_rows, preferred_element_type=jnp.float32
        )
        return (mixture.astype(jnp.bfloat16), logsum[:, :, 0])

    blocks = (
        queries.reshape(block_count, block_rows, head_count, head_depth),
        allowed.reshape(block_count, block_rows, total_rows),
    )
    mixture, logsum = lax.map(one_block, blocks)
    return (mixture.reshape(total_rows, head_count, head_depth), logsum)


def attend_backward(queries, key_rows, value_rows, mixture, grad_mixture, allowed, logsum):
    total_rows, head_count, head_depth = queries.shape
    block_rows = min(512, total_rows)
    block_count = total_rows // block_rows

    def one_block(running, pieces):
        key_grad, value_grad = running
        query_block, mixture_block, grad_block, mask_block, logsum_block = pieces
        scores = jnp.einsum(
            "qhd,khd->hqk", query_block, key_rows, preferred_element_type=jnp.float32
        )
        scores = jnp.where(mask_block[None], scores, NEGATIVE)
        chances = jnp.exp(scores - logsum_block[:, :, None])
        weights = chances.astype(jnp.bfloat16)
        value_grad = value_grad + jnp.einsum(
            "hqk,qhd->khd", weights, grad_block, preferred_element_type=jnp.float32
        )
        weight_grad = jnp.einsum(
            "qhd,khd->hqk", grad_block, value_rows, preferred_element_type=jnp.float32
        )
        row_dot = jnp.sum(
            grad_block.astype(jnp.float32) * mixture_block.astype(jnp.float32), axis=2
        ).T
        score_grad = (chances * (weight_grad - row_dot[:, :, None])).astype(jnp.bfloat16)
        query_grad = jnp.einsum(
            "hqk,khd->qhd", score_grad, key_rows, preferred_element_type=jnp.float32
        )
        key_grad = key_grad + jnp.einsum(
            "hqk,qhd->khd", score_grad, query_block, preferred_element_type=jnp.float32
        )
        return ((key_grad, value_grad), query_grad)

    empty = jnp.zeros((total_rows, head_count, head_depth), jnp.float32)
    pieces = (
        queries.reshape(block_count, block_rows, head_count, head_depth),
        mixture.reshape(block_count, block_rows, head_count, head_depth),
        grad_mixture.reshape(block_count, block_rows, head_count, head_depth),
        allowed.reshape(block_count, block_rows, total_rows),
        logsum,
    )
    (key_grad, value_grad), query_grad = lax.scan(one_block, (empty, empty), pieces)
    return (query_grad.reshape(total_rows, head_count, head_depth), key_grad, value_grad)


def shards(
    inputs,
    segments,
    padding,
    first_gain,
    first_shift,
    second_gain,
    second_shift,
    joint_weight,
    joint_bias,
    dense_weight,
    dense_bias,
    expand_weight,
    expand_bias,
    reduce_weight,
    reduce_bias,
    cotangent,
):
    local_rows = inputs.shape[0] // MICRO
    head_count = joint_weight.shape[1] // (3 * HD)
    query_scale = HD ** (-0.5)
    totals = None
    outputs = []
    back_rows = []
    for micro_index in range(MICRO):
        row_start = micro_index * local_rows
        row_stop = row_start + local_rows
        forward_set = (
            lax.all_gather(joint_weight, "dp", axis=0, tiled=True),
            lax.all_gather(joint_bias, "dp", axis=0, tiled=True),
            lax.all_gather(dense_weight, "dp", axis=1, tiled=True),
            lax.all_gather(dense_bias, "dp", axis=0, tiled=True),
            lax.all_gather(expand_weight, "dp", axis=0, tiled=True),
            lax.all_gather(expand_bias, "dp", axis=0, tiled=True),
            lax.all_gather(reduce_weight, "dp", axis=1, tiled=True),
            lax.all_gather(reduce_bias, "dp", axis=0, tiled=True),
            lax.all_gather(first_gain, "dp", axis=0, tiled=True),
            lax.all_gather(first_shift, "dp", axis=0, tiled=True),
            lax.all_gather(second_gain, "dp", axis=0, tiled=True),
            lax.all_gather(second_shift, "dp", axis=0, tiled=True),
        )
        (
            joint_full,
            joint_bias_full,
            dense_full,
            dense_bias_full,
            expand_full,
            expand_bias_full,
            reduce_full,
            reduce_bias_full,
            gain_one,
            shift_one,
            gain_two,
            shift_two,
        ) = forward_set
        rows_in = inputs[row_start:row_stop].astype(jnp.float32)
        normed, scale_inv = normalize(rows_in)
        hidden_one = (normed * gain_one.astype(jnp.float32) + shift_one.astype(jnp.float32)).astype(
            jnp.bfloat16
        )
        hidden_two = (normed * gain_two.astype(jnp.float32) + shift_two.astype(jnp.float32)).astype(
            jnp.bfloat16
        )
        positions, allowed = layout(segments[row_start:row_stop])
        cosine_table, sine_table = rotary_tables(positions)
        joint = (
            jnp.dot(hidden_one, joint_full, preferred_element_type=jnp.float32)
            + joint_bias_full.astype(jnp.float32)
        ).reshape(local_rows, head_count, 3, HD)
        queries = (rotate(joint[:, :, 0], cosine_table, sine_table) * query_scale).astype(
            jnp.bfloat16
        )
        key_rows = rotate(joint[:, :, 1], cosine_table, sine_table).astype(jnp.bfloat16)
        value_rows = joint[:, :, 2].astype(jnp.bfloat16)
        mixture, logsum = attend_forward(queries, key_rows, value_rows, allowed)
        mixture_flat = mixture.reshape(local_rows, head_count * HD)
        before = jnp.dot(
            hidden_two, expand_full, preferred_element_type=jnp.float32
        ) + expand_bias_full.astype(jnp.float32)
        activated = gelu_value(before).astype(jnp.bfloat16)
        branch_part = jnp.dot(
            mixture_flat, dense_full, preferred_element_type=jnp.float32
        ) + jnp.dot(activated, reduce_full, preferred_element_type=jnp.float32)
        branches = lax.psum(branch_part.astype(jnp.bfloat16), "mp").astype(jnp.float32)
        outputs.append(
            (
                rows_in
                + branches
                + dense_bias_full.astype(jnp.float32)
                + reduce_bias_full.astype(jnp.float32)
            ).astype(jnp.bfloat16)
        )
        joint_again, dense_again, expand_again, reduce_again, first_again, second_again = (
            lax.all_gather(joint_weight, "dp", axis=0, tiled=True),
            lax.all_gather(dense_weight, "dp", axis=1, tiled=True),
            lax.all_gather(expand_weight, "dp", axis=0, tiled=True),
            lax.all_gather(reduce_weight, "dp", axis=1, tiled=True),
            lax.all_gather(first_gain, "dp", axis=0, tiled=True),
            lax.all_gather(second_gain, "dp", axis=0, tiled=True),
        )
        seed_grad = (
            cotangent[row_start:row_stop].astype(jnp.float32)
            * padding[row_start:row_stop].astype(jnp.float32)[:, None]
        )
        seed_low = seed_grad.astype(jnp.bfloat16)
        bias_grad = jnp.sum(seed_grad, axis=0)
        grad_mixture = (
            jnp.dot(seed_low, dense_again.T, preferred_element_type=jnp.float32)
            .astype(jnp.bfloat16)
            .reshape(local_rows, head_count, HD)
        )
        before_grad = jnp.dot(
            seed_low, reduce_again.T, preferred_element_type=jnp.float32
        ) * gelu_slope(before)
        before_low = before_grad.astype(jnp.bfloat16)
        query_grad, key_grad, value_grad = attend_backward(
            queries, key_rows, value_rows, mixture, grad_mixture, allowed, logsum
        )
        joint_grad = jnp.stack(
            [
                unrotate(query_grad * query_scale, cosine_table, sine_table),
                unrotate(key_grad, cosine_table, sine_table),
                value_grad,
            ],
            axis=2,
        ).reshape(local_rows, 3 * head_count * HD)
        joint_low = joint_grad.astype(jnp.bfloat16)
        grad_one, grad_two = (
            lax.psum(
                jnp.dot(joint_low, joint_again.T, preferred_element_type=jnp.float32).astype(
                    jnp.bfloat16
                ),
                "mp",
            ).astype(jnp.float32),
            lax.psum(
                jnp.dot(before_low, expand_again.T, preferred_element_type=jnp.float32).astype(
                    jnp.bfloat16
                ),
                "mp",
            ).astype(jnp.float32),
        )
        grad_normed = grad_one * first_again.astype(jnp.float32) + grad_two * second_again.astype(
            jnp.float32
        )
        back_rows.append(
            (
                seed_grad
                + scale_inv
                * (
                    grad_normed
                    - jnp.mean(grad_normed, axis=1, keepdims=True)
                    - normed * jnp.mean(grad_normed * normed, axis=1, keepdims=True)
                )
            ).astype(jnp.bfloat16)
        )
        terms = (
            jnp.sum(grad_one * normed, axis=0),
            jnp.sum(grad_one, axis=0),
            jnp.sum(grad_two * normed, axis=0),
            jnp.sum(grad_two, axis=0),
            jnp.dot(hidden_one.T, joint_low, preferred_element_type=jnp.float32),
            jnp.sum(joint_grad, axis=0),
            jnp.dot(mixture_flat.T, seed_low, preferred_element_type=jnp.float32),
            bias_grad,
            jnp.dot(hidden_two.T, before_low, preferred_element_type=jnp.float32),
            jnp.sum(before_grad, axis=0),
            jnp.dot(activated.T, seed_low, preferred_element_type=jnp.float32),
            bias_grad,
        )
        totals = (
            terms
            if totals is None
            else tuple((older + newer for older, newer in zip(totals, terms)))
        )
    totals = (
        lax.psum_scatter(
            totals[0].astype(jnp.bfloat16), "dp", scatter_dimension=0, tiled=True
        ).astype(jnp.float32),
        lax.psum_scatter(
            totals[1].astype(jnp.bfloat16), "dp", scatter_dimension=0, tiled=True
        ).astype(jnp.float32),
        lax.psum_scatter(
            totals[2].astype(jnp.bfloat16), "dp", scatter_dimension=0, tiled=True
        ).astype(jnp.float32),
        lax.psum_scatter(
            totals[3].astype(jnp.bfloat16), "dp", scatter_dimension=0, tiled=True
        ).astype(jnp.float32),
        lax.psum_scatter(
            totals[4].astype(jnp.bfloat16), "dp", scatter_dimension=0, tiled=True
        ).astype(jnp.float32),
        lax.psum_scatter(
            totals[5].astype(jnp.bfloat16), "dp", scatter_dimension=0, tiled=True
        ).astype(jnp.float32),
        lax.psum_scatter(
            totals[6].astype(jnp.bfloat16), "dp", scatter_dimension=1, tiled=True
        ).astype(jnp.float32),
        lax.psum_scatter(
            totals[7].astype(jnp.bfloat16), "dp", scatter_dimension=0, tiled=True
        ).astype(jnp.float32),
        lax.psum_scatter(
            totals[8].astype(jnp.bfloat16), "dp", scatter_dimension=0, tiled=True
        ).astype(jnp.float32),
        lax.psum_scatter(
            totals[9].astype(jnp.bfloat16), "dp", scatter_dimension=0, tiled=True
        ).astype(jnp.float32),
        lax.psum_scatter(
            totals[10].astype(jnp.bfloat16), "dp", scatter_dimension=1, tiled=True
        ).astype(jnp.float32),
        lax.psum_scatter(
            totals[11].astype(jnp.bfloat16), "dp", scatter_dimension=0, tiled=True
        ).astype(jnp.float32),
    )
    return (
        jnp.concatenate(outputs, axis=0),
        jnp.concatenate(back_rows, axis=0),
        totals[0],
        totals[1],
        totals[2],
        totals[3],
        totals[4],
        totals[5],
        totals[6],
        totals[7],
        totals[8],
        totals[9],
        totals[10],
        totals[11],
    )


def solution(mesh):
    placed = (
        P("dp", None),
        P("dp"),
        P("dp"),
        P("dp"),
        P("dp"),
        P("dp"),
        P("dp"),
        P("dp", "mp"),
        P(("mp", "dp")),
        P("mp", "dp"),
        P("dp"),
        P("dp", "mp"),
        P(("mp", "dp")),
        P("mp", "dp"),
        P("dp"),
        P("dp", None),
    )
    return jax.shard_map(
        shards,
        mesh=mesh,
        in_specs=placed,
        out_specs=(
            P("dp", None),
            P("dp", None),
            P("dp"),
            P("dp"),
            P("dp"),
            P("dp"),
            P("dp", "mp"),
            P(("mp", "dp")),
            P("mp", "dp"),
            P("dp"),
            P("dp", "mp"),
            P(("mp", "dp")),
            P("mp", "dp"),
            P("dp"),
        ),
        check_vma=False,
    )
```

profile of v0, /device:TPU:0, one launch (start us, length us, event | category | flops | bytes accessed | tf_op | source)
XLA Modules:
  0.0 900.3 jit_solution(295608793468583112)
XLA Ops:
  16.2 15.3 %all-reduce = bf16[1536]{0:T(1024)(128)(2,1)S(1)} all-reduce(bf16[1536]{0:T(1024)(128)(2,1)S(1)} %dynamic-update-slice), channel_id=1, replica_groups=mesh['dp'=8,'mp'=4] {'dp'}, use_global_device_ids=true, to_apply=%add | all-reduce | flops 1536 | bytes 6144
  32.7 8.3 all-gather.4
  41.0 8.9 all-gather.3
  49.9 8.2 all-gather.2
  58.0 8.9 all-gather.1
  66.9 8.3 all-gather
  75.3 2.9 convert_reduce_fusion.5
  78.2 1.5 fusion.31
  80.8 3.0 multiply_cosine_fusion.1
  83.8 4.6 convolution_convert_fusion.5
  88.3 2.2 convolution_convert_fusion.4
  90.5 8.6 convolution_add_fusion
  99.1 2.7 copy.99
  101.7 1.6 fusion.115
  103.4 2.6 copy.156
  106.0 2.2 slice.262
  108.2 1.7 copy.155
  112.8 1.6 multiply_reduce_fusion
  120.2 5.1 convolution_add_fusion.1
  125.4 3.8 copy.94
  129.2 2.8 fusion.114
  133.3 1.6 copy.153
  143.5 1.7 multiply_add_fusion.1
  147.0 2.8 add_convert_fusion.3
  149.9 1.8 maximum_bitcast_fusion.3
  151.7 2.7 maximum_bitcast_fusion.2
  155.4 1.5 fusion.61
  156.9 3.0 copy.127
  166.1 9.5 %fusion.94 = f32[2048,1536]{1,0:T(8,128)} fusion(bf16[512,1536]{0,1:T(8,128)(2,1)S(1)} %bitcast.127, f32[2048]{0:T(1024)S(1)} %bitcast.161, f32[2048]{0:T(1024)S(1)} %bitcast.142, f32[512]{0:T(512)S(1)} %add_rsqrt_fusion.1, f32[512]{0:T(512)S(1)} %broadcast_multiply_fusion.5, bf16[1024,2048]{1,0:T(8,128)(2,1)} %param.16), kind=kOutput, calls=%fused_computation.213 | convolution fusion | flops 3227516928 | bytes 16273408 | tf_op jit(solution)/shard_map/dot_general | solution.py:312
  175.6 8.9 add_convert_fusion.2
  184.6 7.5 convolution_convert_fusion.1
  192.2 7.6 convolution_convert_fusion.3
  199.8 10.6 %fusion.98 = f32[512,2048]{1,0:T(8,128)} fusion(bf16[2048,2048]{1,0:T(8,128)(2,1)} %all-gather.16.cloned.1.call-done, f32[512]{0:T(512)S(1)} %add_rsqrt_fusion, f32[512]{0:T(512)S(1)} %broadcast_multiply_fusion.4, f32[2048]{0:T(1024)S(1)} %bitcast.149, f32[2048]{0:T(1024)S(1)} %bitcast.133, bf16[1024,2048]{1,0:T(8,128)(2,1)} %param.16), kind=kOutput, calls=%fused_computation.214 | convolution fusion | flops 4301258752 | bytes 14700544 | tf_op jit(solution)/shard_map/dot_general | solution.py:228
  210.4 9.9 %fusion.112 = f32[512,2048]{1,0:T(8,128)S(1)} fusion(bf16[2048,2048]{1,0:T(8,128)(2,1)} %all-gather.18.cloned.1.call-done, f32[512,2048]{1,0:T(8,128)} %fusion.98, f32[2048]{0:T(1024)S(1)} %bitcast.153), kind=kOutput, calls=%fused_computation.217 | convolution fusion | flops 4301258752 | bytes 16785408 | tf_op jit(solution)/shard_map/dot_general | solution.py:234
  220.4 2.7 add_convert_fusion.4
  223.1 4.6 fusion.92
  227.7 2.0 copy-done.64
  229.7 4.8 fusion.113
  234.5 2.7 add_convert_fusion.5
  237.2 8.8 fusion.119
  246.0 7.7 convolution_convert_fusion
  253.7 9.1 %fusion.118 = (f32[2048]{0:T(1024)S(1)}, bf16[512,2048]{1,0:T(8,128)(2,1)}) fusion(f32[512,2048]{1,0:T(8,128)} %copy-done.64, f32[2048]{0:T(1024)S(1)} %bitcast.156, bf16[2048,2048]{1,0:T(8,128)(2,1)S(1)} %bitcast.164, f32[512]{0:T(512)S(1)} %get-tuple-element.188, bf16[1024,2048]{1,0:T(8,128)(2,1)S(1)} %copy-done.8), kind=kOutput, calls=%fused_computation.223 | convolution fusion | flops 4310693888 | bytes 16795648 | tf_op jit(solution)/shard_map/dot_general | solution.py:263
  262.8 8.1 convolution_convert_fusion.2
  271.0 14.0 %fusion.102 = f32[2048,2048]{1,0:T(8,128)} fusion(f32[512]{0:T(512)S(1)} %get-tuple-element.188, bf16[1024,2048]{1,0:T(8,128)(2,1)} %param.31, f32[512,2048]{1,0:T(8,128)} %copy-done.64, f32[2048]{0:T(1024)S(1)} %bitcast.157), kind=kOutput, calls=%fused_computation.215 | convolution fusion | flops 4304404480 | bytes 23078912 | tf_op jit(solution)/shard_map/dot_general | solution.py:318
  285.1 10.6 %add_convert_fusion = bf16[2048,2048]{1,0:T(8,128)(2,1)} fusion(f32[2048,2048]{1,0:T(8,128)} %fusion.102, f32[512]{0:T(512)S(1)} %get-tuple-element.189, bf16[1024,2048]{1,0:T(8,128)(2,1)S(1)} %copy-done.9, f32[512,2048]{1,0:T(8,128)S(1)} %copy-done.65, f32[2048]{0:T(1024)S(1)} %bitcast.158), kind=kOutput, calls=%fused_computation | convolution fusion | flops 4312793088 | bytes 31467520 | tf_op jit(solution)/shard_map/dot_general | solution.py:318
  295.7 1.5 copy-done.66
  297.2 10.4 %fusion.72 = f32[2048,2048]{1,0:T(8,128)} fusion(bf16[512,2048]{1,0:T(8,128)(2,1)S(1)} %copy-done.66, f32[2048]{0:T(1024)S(1)} %bitcast.151, f32[2048]{0:T(1024)S(1)} %bitcast.135, f32[512]{0:T(512)S(1)} %add_rsqrt_fusion.1, f32[512]{0:T(512)S(1)} %broadcast_multiply_fusion.5, bf16[1024,2048]{1,0:T(8,128)(2,1)} %param.16), kind=kOutput, calls=%fused_computation.147 | convolution fusion | flops 4301258752 | bytes 20992000 | tf_op jit(solution)/shard_map/dot_general | solution.py:316
  307.6 11.3 %add_convert_fusion.1 = bf16[2048,2048]{1,0:T(8,128)(2,1)} fusion(f32[2048,2048]{1,0:T(8,128)} %fusion.72, bf16[512,2048]{1,0:T(8,128)(2,1)} %get-tuple-element.211, f32[512]{0:T(512)S(1)} %add_rsqrt_fusion, f32[512]{0:T(512)S(1)} %broadcast_multiply_fusion.4, f32[2048]{0:T(1024)S(1)} %bitcast.152, f32[2048]{0:T(1024)S(1)} %bitcast.136, ...), kind=kOutput, calls=%fused_computation.1 | convolution fusion | flops 4309647360 | bytes 29380608 | tf_op jit(solution)/shard_map/dot_general | solution.py:316
  320.9 8.3 all-gather.6
  329.1 8.6 all-gather.5
  338.0 2.1 fusion.62
  340.1 1.8 convert_element_type.387
  341.9 2.5 convert_element_type.382
  344.4 396.9 %all-reduce.12.cloned.1.call-done = (bf16[512,2048]{1,0:T(8,128)(2,1)}, bf16[512,2048]{1,0:T(8,128)(2,1)}, bf16[512,2048]{1,0:T(8,128)(2,1)}, bf16[512,2048]{1,0...) async-done(((bf16[512,2048]{1,0:T(8,128)(2,1)}, bf16[512,2048]{1,0:T(8,128)(2,1)}, bf16[512,2048]{1,0:T(8,128)(2,1)}, bf16[512,2048]{1,0:T(8,128)(2,1)}, ...) | async-done | bytes 12582928 | tf_op jit(solution)/shard_map/psum | solution.py:235
  741.4 9.7 %fusion.45 = (f32[2048]{0:T(1024)S(1)}, f32[512]{0:T(512)S(1)}, f32[2048]{0:T(1024)S(1)}, f32[2048]{0:T(1024)S(1)}, f32[512]{0:T(512)S(1)}, /*index=5*/f32[2048]...) fusion(bf16[512,2048]{1,0:T(8,128)(2,1)} %get-tuple-element.154, ...), kind=kLoop, calls=%fused_computation.68 | loop fusion | flops 35633152 | bytes 12681216 | tf_op jit(solution)/shard_map/reduce_sum | solution.py:310
  751.1 4.3 fusion.54
  755.5 25.5 %all-reduce.8 = (bf16[2048]{0:T(1024)(128)(2,1)S(1)}, bf16[2048]{0:T(1024)(128)(2,1)S(1)}, bf16[2048]{0:T(1024)(128)(2,1)S(1)}, bf16[2048]{0:T(1024)(128)(2,1)S(...) all-reduce(bf16[2048]{0:T(1024)(128)(2,1)S(1)} %add_convert_fusion., ...), channel_id=2, replica_groups=mesh['dp'=8,'mp'=4] {'dp'}, use_global_device_ids=true, to_apply=%region_24.25.clone | all-reduce | flops 13824 | bytes 55296
  781.1 34.1 %reduce-scatter.11.cloned.1.call-done = bf16[2048,256]{1,0:T(8,128)(2,1)} async-done(((bf16[2048,2048]{1,0:T(8,128)(2,1)}), bf16[2048,256]{1,0:T(8,128)(2,1)}) %reduce-scatter.11.cloned.1.call-update) | async-done | bytes 1048592 | tf_op jit(solution)/shard_map/reduce_scatter | solution.py:357
  815.2 2.7 convert_element_type.395
  821.7 8.1 fusion.34
  829.9 2.9 pad_maximum_fusion
  832.8 2.6 pad_maximum_fusion.1
  835.4 54.8 %reduce-scatter.9.cloned.1.call-done = bf16[256,2048]{1,0:T(8,128)(2,1)} async-done(((bf16[2048,2048]{1,0:T(8,128)(2,1)}), bf16[256,2048]{1,0:T(8,128)(2,1)}) %reduce-scatter.9.cloned.1.call-update) | async-done | bytes 1048592 | tf_op jit(solution)/shard_map/reduce_scatter | solution.py:351
  890.2 2.8 convert_element_type.391
  (250 shorter events, 43.0 us)
Async XLA Ops:
  7.2 76.6 %all-gather.14.cloned.1.call-start = ((), (), s32[]{:S(2)}) async-start(), calls=%async_computation.5 | async-start | bytes 2359296 | tf_op jit(solution)/shard_map/all_gather | solution.py:182
  7.9 82.6 %all-gather.12.cloned.1.call-start = ((), (), s32[]{:S(2)}) async-start(), calls=%async_computation.4 | async-start | bytes 7077888 | tf_op jit(solution)/shard_map/all_gather | solution.py:180
  8.7 191.2 %all-gather.16.cloned.1.call-start = ((), (), s32[]{:S(2)}) async-start(), calls=%async_computation.6 | async-start | bytes 9437184 | tf_op jit(solution)/shard_map/all_gather | solution.py:184
  9.4 201.0 %all-gather.18.cloned.1.call-start = ((), (), s32[]{:S(2)}) async-start(), calls=%async_computation.7 | async-start | bytes 9437184 | tf_op jit(solution)/shard_map/all_gather | solution.py:186
  10.0 330.1 %reduce-scatter.7.cloned.1.call-start = ((), (), s32[]{:S(2)}) async-start(), calls=%async_computation.9 | async-start | bytes 2359296 | tf_op jit(solution)/shard_map/reduce_scatter | solution.py:345
  31.5 46.6 %copy-start = (bf16[1024,2048]{1,0:T(8,128)(2,1)S(1)}, bf16[1024,2048]{1,0:T(8,128)(2,1)}, u32[]{:S(2)}) copy-start(bf16[1024,2048]{1,0:T(8,128)(2,1)} %param.16) | copy-start | bytes 12582916
  75.2 100.4 %copy-start.57 = (f32[8,1,256]{2,1,0:T(1,128)}, f32[8,1,256]{2,1,0:T(1,128)S(1)}, u32[]{:S(2)}) copy-start(f32[8,1,256]{2,1,0:T(1,128)S(1)} %convert_element_type.396) | copy-start | bytes 24580
  75.2 4.4 copy-start.59
  83.8 4.6 copy-start.6
  83.8 4.6 copy-start.34
  101.7 6.5 copy-start.24
  108.2 2.1 copy-start.36
  108.2 2.1 copy-start.46
  108.2 2.1 copy-start.48
  110.8 2.0 copy-start.55
  112.2 3.0 copy-start.32
  112.2 8.0 slice-start.2
  114.4 5.8 slice-start.3
  116.7 3.6 copy-start.1
  134.9 2.4 copy-start.51
  136.6 2.0 copy-start.23
  136.6 2.1 copy-start.53
  138.0 2.4 copy-start.30
  139.5 5.7 copy-start.40
  140.4 3.1 copy-start.21
  140.4 3.1 copy-start.47
  140.4 3.1 copy-start.49
  142.1 12.3 %copy-start.11 = (f32[512,2,1,256]{3,0,1,2:T(8,128)}, f32[512,2,1,256]{3,0,1,2:T(8,128)S(1)}, u32[]{:S(2)}) copy-start(f32[512,2,1,256]{3,0,1,2:T(8,128)S(1)} %convolution_bitcast_fusion.2) | copy-start | bytes 3145732
  142.1 3.5 copy-start.7
  147.0 2.9 copy-start.37
  149.8 192.1 %reduce-scatter.5.cloned.1.call-start = ((), (), s32[]{:S(2)}) async-start(), calls=%async_computation.8 | async-start | bytes 7077888 | tf_op jit(solution)/shard_map/reduce_scatter | solution.py:339
  151.7 2.7 copy-start.13
  155.4 4.5 copy-start.22
  156.9 3.7 copy-start.44
  156.9 3.7 copy-start.45
  161.1 2.0 copy-start.54
  166.1 9.5 %copy-start.2 = (bf16[1024,2048]{1,0:T(8,128)(2,1)S(1)}, bf16[1024,2048]{1,0:T(8,128)(2,1)}, u32[]{:S(2)}) copy-start(bf16[1024,2048]{1,0:T(8,128)(2,1)} %param.16) | copy-start | bytes 12582916
  166.1 9.5 %copy-start.52 = (bf16[512,2,3,256]{0,3,2,1:T(8,128)(2,1)S(1)}, bf16[512,2,3,256]{0,3,2,1:T(8,128)(2,1)}, u32[]{:S(2)}) copy-start(bf16[512,2,3,256]{0,3,2,1:T(8,128)(2,1)} %copy.127) | copy-start | bytes 4718596
  184.6 556.8 %all-reduce.12.cloned.1.call-start = ((), (), s32[]{:S(2)}) async-start(), calls=%async_computation.12 | async-start | bytes 25165824 | tf_op jit(solution)/shard_map/psum | solution.py:235
  210.4 9.9 %copy-start.35 = (bf16[512,2048]{1,0:T(8,128)(2,1)S(1)}, bf16[512,2048]{1,0:T(8,128)(2,1)}, u32[]{:S(2)}) copy-start(bf16[512,2048]{1,0:T(8,128)(2,1)} %all-gather.14.cloned.1.call-done) | copy-start | bytes 6291460
  210.4 9.9 %copy-start.39 = (bf16[2,256,512]{2,1,0:T(8,128)(2,1)S(1)}, bf16[2,256,512]{2,1,0:T(8,128)(2,1)}, u32[]{:S(2)}) copy-start(bf16[2,256,512]{2,1,0:T(8,128)(2,1)} %get-tuple-element.205) | copy-start | bytes 1572868
  210.4 12.6 %copy-start.61 = (bf16[2048,2048]{1,0:T(8,128)(2,1)S(1)}, bf16[2048,2048]{1,0:T(8,128)(2,1)}, u32[]{:S(2)}) copy-start(bf16[2048,2048]{1,0:T(8,128)(2,1)} %all-gather.16.cloned.1.call-done) | copy-start | bytes 25165828
  220.3 2.7 copy-start.3
  220.4 9.4 %slice-start = ((s8[8388608]{0:T(1024)(128)(4,1)}), s8[4194304]{0:T(1024)(128)(4,1)S(1)}, s32[]{:S(2)}) async-start(s8[8388608]{0:T(1024)(128)(4,1)} %bitcast.163), calls=%async_computation.13 | async-start | bytes 8388608
  223.1 6.7 slice-start.1
  227.7 2.0 copy-start.64
  229.7 4.8 copy-start.41
  234.5 2.7 copy-start.8
  270.9 544.3 %reduce-scatter.11.cloned.1.call-start = ((), (), s32[]{:S(2)}) async-start(), calls=%async_computation.11 | async-start | bytes 9437184 | tf_op jit(solution)/shard_map/reduce_scatter | solution.py:357
  271.0 14.0 %copy-start.9 = (bf16[1024,2048]{1,0:T(8,128)(2,1)S(1)}, bf16[1024,2048]{1,0:T(8,128)(2,1)}, u32[]{:S(2)}) copy-start(bf16[1024,2048]{1,0:T(8,128)(2,1)} %param.31) | copy-start | bytes 12582916
  271.0 14.0 %copy-start.65 = (f32[512,2048]{1,0:T(8,128)S(1)}, f32[512,2048]{1,0:T(8,128)}, u32[]{:S(2)}) copy-start(f32[512,2048]{1,0:T(8,128)} %fusion.98) | copy-start | bytes 12582916
  295.7 594.5 %reduce-scatter.9.cloned.1.call-start = ((), (), s32[]{:S(2)}) async-start(), calls=%async_computation.10 | async-start | bytes 9437184 | tf_op jit(solution)/shard_map/reduce_scatter | solution.py:351
  297.2 10.4 %copy-start.4 = (bf16[1024,2048]{1,0:T(8,128)(2,1)S(1)}, bf16[1024,2048]{1,0:T(8,128)(2,1)}, u32[]{:S(2)}) copy-start(bf16[1024,2048]{1,0:T(8,128)(2,1)} %param.16) | copy-start | bytes 12582916
  318.9 18.9 %copy-start.12 = (f32[512,2,1,256]{3,0,1,2:T(8,128)S(1)}, f32[512,2,1,256]{3,0,1,2:T(8,128)}, u32[]{:S(2)}) copy-start(f32[512,2,1,256]{3,0,1,2:T(8,128)} %copy-done.11) | copy-start | bytes 3145732
  318.9 18.9 %copy-start.14 = (f32[512,2,1,256]{3,0,1,2:T(8,128)S(1)}, f32[512,2,1,256]{3,0,1,2:T(8,128)}, u32[]{:S(2)}) copy-start(f32[512,2,1,256]{3,0,1,2:T(8,128)} %copy-done.13) | copy-start | bytes 3145732
  318.9 18.9 %copy-start.16 = (f32[512,2,1,256]{3,0,1,2:T(8,128)S(1)}, f32[512,2,1,256]{3,0,1,2:T(8,128)}, u32[]{:S(2)}) copy-start(f32[512,2,1,256]{3,0,1,2:T(8,128)} %copy-done.15) | copy-start | bytes 3145732
  337.8 403.6 %copy-start.58 = (f32[8,1,256]{2,1,0:T(1,128)S(1)}, f32[8,1,256]{2,1,0:T(1,128)}, u32[]{:S(2)}) copy-start(f32[8,1,256]{2,1,0:T(1,128)} %copy-done.57) | copy-start | bytes 24580
  741.4 9.7 %copy-start.5 = (bf16[1024,2048]{1,0:T(8,128)(2,1)S(1)}, bf16[1024,2048]{1,0:T(8,128)(2,1)}, u32[]{:S(2)}) copy-start(bf16[1024,2048]{1,0:T(8,128)(2,1)} %param.16) | copy-start | bytes 12582916
  741.4 9.8 %copy-start.10 = (bf16[1024,2048]{1,0:T(8,128)(2,1)S(1)}, bf16[1024,2048]{1,0:T(8,128)(2,1)}, u32[]{:S(2)}) copy-start(bf16[1024,2048]{1,0:T(8,128)(2,1)} %param.31) | copy-start | bytes 12582916
  741.4 9.8 %copy-start.27 = (bf16[512,2048]{1,0:T(8,128)(2,1)S(1)}, bf16[512,2048]{1,0:T(8,128)(2,1)}, u32[]{:S(2)}) copy-start(bf16[512,2048]{1,0:T(8,128)(2,1)} %get-tuple-element.154) | copy-start | bytes 6291460
  741.4 9.8 %copy-start.28 = (bf16[512,2048]{1,0:T(8,128)(2,1)S(1)}, bf16[512,2048]{1,0:T(8,128)(2,1)}, u32[]{:S(2)}) copy-start(bf16[512,2048]{1,0:T(8,128)(2,1)} %get-tuple-element.155) | copy-start | bytes 6291460
  755.5 66.3 %copy-start.26 = (bf16[512,2048]{1,0:T(8,128)(2,1)S(1)}, bf16[512,2048]{1,0:T(8,128)(2,1)}, u32[]{:S(2)}) copy-start(bf16[512,2048]{1,0:T(8,128)(2,1)} %get-tuple-element.152) | copy-start | bytes 6291460
  781.1 111.9 %copy-start.60 = (f32[256]{0:T(256)}, f32[256]{0:T(256)S(1)}, u32[]{:S(2)}) copy-start(f32[256]{0:T(256)S(1)} %dynamic-slice_convert_fusion.1) | copy-start | bytes 3076
  829.9 2.9 copy-start.29
  (16 other events, 25.4 us)
Sparse Core Ops, SparseCore 0:
  9.9 30.8 all-gather.13
  42.7 45.4 all-gather.11
  90.0 54.2 all-gather.15
  146.1 55.8 all-gather.17
  205.1 41.1 reduce-scatter.6
  249.5 61.7 reduce-scatter.4
  315.1 426.1 all-reduce.11
  744.8 70.3 reduce-scatter.10
  818.7 71.4 reduce-scatter.8
where the time goes:
time: 908 us; the launch traced here: 900 us
  waiting for transfers between devices  489 us (54%)
  matrix products  184 us (20%)
  blocking collectives  100 us (11%)
  other arithmetic  66.2 us (7%)
  local copies, waits for them, and re-layouts  43.6 us (5%)
  between operations  17.7 us (2%)
    psum x1, waiting for transfers between devices, shards(): lax.psum(branch_part.astype(jnp.bfloat16), 'mp').astype(jnp.float32)  397 us
    reduce_scatter x1, waiting for transfers between devices, shards(): lax.psum_scatter(totals[8].astype(jnp.bfloat16), 'dp', scatter_dimension=...  54.8 us
    unnamed x2, blocking collectives  40.8 us
    reduce_scatter x1, waiting for transfers between devices, shards(): lax.psum_scatter(totals[10].astype(jnp.bfloat16), 'dp', scatter_dimension...  34.1 us
    dot_general x2, matrix products, shards(): jnp.dot(activated.T, seed_low, preferred_element_type=jnp.float32)  24.6 us
    dot_general x2, matrix products, shards(): jnp.dot(hidden_two.T, before_low, preferred_element_type=jnp.float32)  21.7 us
    unnamed x157, local copies, waits for them, and re-layouts  20.9 us
    dot_general x2, matrix products, shards(): jnp.dot(hidden_one.T, joint_low, preferred_element_type=jnp.float32)  18.4 us
  transfers between devices with their start and end apart: 9, of which 3 were waited for; matrix products, arithmetic and copies ran while one was open for 31% of the time, Pallas kernels for 0%

commit v1 on v0

--- a/solution.py
+++ b/solution.py
@@ -232,7 +232,9 @@
         branch_part = jnp.dot(
             mixture_flat, dense_full, preferred_element_type=jnp.float32
         ) + jnp.dot(activated, reduce_full, preferred_element_type=jnp.float32)
-        branches = lax.psum(branch_part.astype(jnp.bfloat16), "mp").astype(jnp.float32)
+        branches = jnp.sum(lax.all_gather(branch_part.astype(jnp.bfloat16), "mp"), axis=0).astype(
+            jnp.float32
+        )
         outputs.append(
             (
                 rows_in

time: 908 us -> 1070 us (1.18)
  waiting for transfers between devices: 489 us -> 633 us
  other arithmetic: 66.2 us -> 80.5 us
    all_gather x0 -> x2, waiting for transfers between devices: none -> 249 us  [shards(): lax.all_gather(branch_part.astype(jnp.bfloat16), 'mp')]
    psum x1, waiting for transfers between devices: 397 us -> 257 us  [shards(): lax.psum(jnp.dot(before_low, expand_again.T, preferred_element_type=jnp.f...]
    reduce_scatter x1, waiting for transfers between devices: 34.1 us -> 65.6 us  [shards(): lax.psum_scatter(totals[10].astype(jnp.bfloat16), 'dp', scatter_dimension...]
    reduce_sum x0 -> x2, other arithmetic: none -> 14.4 us  [shards(): jnp.sum(lax.all_gather(branch_part.astype(jnp.bfloat16), 'mp'), axis=0)]
    unnamed x157 -> x159, local copies, waits for them, and re-layouts: 20.9 us -> 21.7 us
  transfers between devices with their start and end apart: 9 -> 11, of which waited for: 3 -> 5; matrix products, arithmetic and copies ran while one was open for 31% -> 28% of each run, Pallas kernels for 0% -> 0%
where the time goes in v1:
time: 1070 us; the launch traced here: 1060 us
  waiting for transfers between devices  633 us (59%)
  matrix products  186 us (17%)
  blocking collectives  102 us (10%)
  other arithmetic  80.5 us (8%)
  local copies, waits for them, and re-layouts  44.3 us (4%)
  between operations  17.6 us (2%)
    psum x1, waiting for transfers between devices, shards(): lax.psum(jnp.dot(before_low, expand_again.T, preferred_element_type=jnp.f...  257 us
    all_gather x2, waiting for transfers between devices, shards(): lax.all_gather(branch_part.astype(jnp.bfloat16), 'mp')  249 us
    reduce_scatter x1, waiting for transfers between devices, shards(): lax.psum_scatter(totals[10].astype(jnp.bfloat16), 'dp', scatter_dimension...  65.6 us
    reduce_scatter x1, waiting for transfers between devices, shards(): lax.psum_scatter(totals[8].astype(jnp.bfloat16), 'dp', scatter_dimension=...  58.8 us
    unnamed x2, blocking collectives  41.3 us
    dot_general x2, matrix products, shards(): jnp.dot(activated.T, seed_low, preferred_element_type=jnp.float32)  24.3 us
    unnamed x159, local copies, waits for them, and re-layouts  21.7 us
    dot_general x2, matrix products, shards(): jnp.dot(hidden_two.T, before_low, preferred_element_type=jnp.float32)  21.6 us
  transfers between devices with their start and end apart: 11, of which 5 were waited for; matrix products, arithmetic and copies ran while one was open for 28% of the time, Pallas kernels for 0%

profile of v1, /device:TPU:0, one launch (start us, length us, event | category | flops | bytes accessed | tf_op | source)
XLA Modules:
  0.0 1063.9 jit_solution(8010743790089606844)
XLA Ops:
  16.2 15.3 %all-reduce = bf16[1536]{0:T(1024)(128)(2,1)S(1)} all-reduce(bf16[1536]{0:T(1024)(128)(2,1)S(1)} %dynamic-update-slice), channel_id=1, replica_groups=mesh['dp'=8,'mp'=4] {'dp'}, use_global_device_ids=true, to_apply=%add | all-reduce | flops 1536 | bytes 6144
  32.7 8.3 all-gather.6
  41.0 8.9 all-gather.5
  49.9 8.2 all-gather.4
  58.0 8.9 all-gather.3
  66.9 8.3 all-gather.2
  75.3 2.9 convert_reduce_fusion.5
  80.8 3.0 multiply_cosine_fusion.1
  83.7 4.6 convolution_convert_fusion.5
  88.3 2.2 convolution_convert_fusion.4
  90.5 8.6 convolution_add_fusion
  99.1 2.7 copy.99
  101.8 1.6 fusion.115
  103.4 2.7 copy.156
  106.0 2.2 slice.262
  108.3 1.7 copy.155
  112.8 1.6 multiply_reduce_fusion
  120.2 5.1 convolution_add_fusion.1
  125.4 4.0 copy.94
  129.3 2.8 fusion.114
  143.6 1.7 multiply_add_fusion.1
  147.2 2.8 add_convert_fusion.3
  150.0 1.8 maximum_bitcast_fusion.3
  151.8 2.7 maximum_bitcast_fusion.2
  157.1 2.8 copy.127
  166.1 9.5 fusion.94
  175.6 9.0 add_convert_fusion.2
  184.7 7.7 convolution_convert_fusion.1
  192.4 7.5 convolution_convert_fusion.3
  199.9 10.6 fusion.98
  210.5 10.1 fusion.119
  221.9 5.8 convolution_convert_fusion
  227.7 6.7 fusion.92
  234.3 8.0 fusion.118
  243.8 5.8 convolution_convert_fusion.2
  249.7 9.3 fusion.113
  259.0 2.7 add_convert_fusion.5
  261.9 9.8 fusion.112
  271.8 2.8 add_convert_fusion.4
  274.7 13.6 %fusion.102 = f32[2048,2048]{1,0:T(8,128)} fusion(f32[512]{0:T(512)S(1)} %get-tuple-element.186, bf16[1024,2048]{1,0:T(8,128)(2,1)} %param.31, f32[512,2048]{1,0:T(8,128)} %fusion.92, f32[2048]{0:T(1024)S(1)} %bitcast.161), kind=kOutput, calls=%fused_computation.215 | convolution fusion | flops 4304404480 | bytes 23078912 | tf_op jit(solution)/shard_map/dot_general | solution.py:320
  288.3 10.6 add_convert_fusion
  299.2 1.6 copy-done.66
  300.8 10.3 fusion.72
  311.1 11.3 %add_convert_fusion.1 = bf16[2048,2048]{1,0:T(8,128)(2,1)} fusion(f32[2048,2048]{1,0:T(8,128)} %fusion.72, bf16[512,2048]{1,0:T(8,128)(2,1)} %copy-done.67, f32[512]{0:T(512)S(1)} %add_rsqrt_fusion, f32[512]{0:T(512)S(1)} %broadcast_multiply_fusion.4, f32[2048]{0:T(1024)S(1)} %bitcast.156, f32[2048]{0:T(1024)S(1)} %bitcast.140, ...), kind=kOutput, calls=%fused_computation.1 | convolution fusion | flops 4309647360 | bytes 29380608 | tf_op jit(solution)/shard_map/dot_general | solution.py:318
  324.1 9.3 all-gather.8
  333.4 8.7 all-gather.7
  342.3 2.1 fusion.62
  344.4 1.8 convert_element_type.391
  346.2 2.5 convert_element_type.386
  348.6 257.0 %all-reduce.12.cloned.1.call-done = (bf16[512,2048]{1,0:T(8,128)(2,1)}, bf16[512,2048]{1,0:T(8,128)(2,1)}, bf16[512,2048]{1,0:T(8,128)(2,1)}, bf16[512,2048]{1,0:T(8,128)(2,1)}) async-done(((bf16[512,2048]{1,0:T(8,128)(2,1)}, bf16[512,2048]{1,0:T(8,128)(2,1)}, bf16[512,2048]{1,0:T(8,128)(2,1)}, bf16[512,2048]{1,0:T(8,128)(2,1)}), (bf16[512,2048]{1,0:T(8,128)(2,1)}, bf16[512,2048]{1,0:T(8,128)(2,1)}, ...) | async-done | bytes 8388624 | tf_op jit(solution)/shard_map/psum | solution.py:288
  605.7 9.7 fusion.45
  615.4 4.3 fusion.54
  619.8 25.9 %all-reduce.8 = (bf16[2048]{0:T(1024)(128)(2,1)S(1)}, bf16[2048]{0:T(1024)(128)(2,1)S(1)}, bf16[2048]{0:T(1024)(128)(2,1)S(1)}, bf16[2048]{0:T(1024)(128)(2,1)S(...) all-reduce(bf16[2048]{0:T(1024)(128)(2,1)S(1)} %add_convert_fusion., ...), channel_id=4, replica_groups=mesh['dp'=8,'mp'=4] {'dp'}, use_global_device_ids=true, to_apply=%region_24.25.clone | all-reduce | flops 13824 | bytes 55296
  649.6 106.8 %all-gather.24.cloned.1.call-done = bf16[2048,2048]{1,0:T(8,128)(2,1)} async-done(((bf16[512,2048]{1,0:T(8,128)(2,1)}), bf16[2048,2048]{1,0:T(8,128)(2,1)}) %all-gather.24.cloned.1.call-update) | async-done | bytes 8388624 | tf_op jit(solution)/shard_map/all_gather | solution.py:235
  756.4 7.2 reduce_sum.284
  763.6 142.2 %all-gather.26.cloned.1.call-done = bf16[2048,2048]{1,0:T(8,128)(2,1)} async-done(((bf16[512,2048]{1,0:T(8,128)(2,1)}), bf16[2048,2048]{1,0:T(8,128)(2,1)}) %all-gather.26.cloned.1.call-update) | async-done | bytes 8388624 | tf_op jit(solution)/shard_map/all_gather | solution.py:235
  905.8 7.2 reduce_sum.289
  913.0 65.6 %reduce-scatter.11.cloned.1.call-done = bf16[2048,256]{1,0:T(8,128)(2,1)} async-done(((bf16[2048,2048]{1,0:T(8,128)(2,1)}), bf16[2048,256]{1,0:T(8,128)(2,1)}) %reduce-scatter.11.cloned.1.call-update) | async-done | bytes 1048592 | tf_op jit(solution)/shard_map/reduce_scatter | solution.py:359
  978.6 2.7 convert_element_type.399
  981.3 7.6 fusion.34
  989.0 3.0 pad_maximum_fusion
  992.0 2.8 pad_maximum_fusion.1
  994.8 58.8 %reduce-scatter.9.cloned.1.call-done = bf16[256,2048]{1,0:T(8,128)(2,1)} async-done(((bf16[2048,2048]{1,0:T(8,128)(2,1)}), bf16[256,2048]{1,0:T(8,128)(2,1)}) %reduce-scatter.9.cloned.1.call-update) | async-done | bytes 1048592 | tf_op jit(solution)/shard_map/reduce_scatter | solution.py:353
  1053.6 2.8 convert_element_type.395
  (260 shorter events, 50.7 us)
Async XLA Ops:
  7.2 76.5 %all-gather.18.cloned.1.call-start = ((), (), s32[]{:S(2)}) async-start(), calls=%async_computation.5 | async-start | bytes 2359296 | tf_op jit(solution)/shard_map/all_gather | solution.py:182
  7.9 82.6 %all-gather.16.cloned.1.call-start = ((), (), s32[]{:S(2)}) async-start(), calls=%async_computation.4 | async-start | bytes 7077888 | tf_op jit(solution)/shard_map/all_gather | solution.py:180
  8.7 191.3 %all-gather.20.cloned.1.call-start = ((), (), s32[]{:S(2)}) async-start(), calls=%async_computation.6 | async-start | bytes 9437184 | tf_op jit(solution)/shard_map/all_gather | solution.py:184
  9.4 201.1 %all-gather.22.cloned.1.call-start = ((), (), s32[]{:S(2)}) async-start(), calls=%async_computation.7 | async-start | bytes 9437184 | tf_op jit(solution)/shard_map/all_gather | solution.py:186
  10.0 334.4 %reduce-scatter.7.cloned.1.call-start = ((), (), s32[]{:S(2)}) async-start(), calls=%async_computation.9 | async-start | bytes 2359296 | tf_op jit(solution)/shard_map/reduce_scatter | solution.py:347
  31.5 46.6 %copy-start = (bf16[1024,2048]{1,0:T(8,128)(2,1)S(1)}, bf16[1024,2048]{1,0:T(8,128)(2,1)}, u32[]{:S(2)}) copy-start(bf16[1024,2048]{1,0:T(8,128)(2,1)} %param.16) | copy-start | bytes 12582916
  75.2 100.4 %copy-start.57 = (f32[8,1,256]{2,1,0:T(1,128)}, f32[8,1,256]{2,1,0:T(1,128)S(1)}, u32[]{:S(2)}) copy-start(f32[8,1,256]{2,1,0:T(1,128)S(1)} %convert_element_type.400) | copy-start | bytes 24580
  75.2 4.4 copy-start.59
  83.7 4.6 copy-start.6
  83.7 4.6 copy-start.34
  101.8 6.5 copy-start.24
  108.3 2.1 copy-start.36
  108.3 2.1 copy-start.46
  108.3 2.1 copy-start.48
  110.8 2.0 copy-start.55
  112.3 3.0 copy-start.32
  112.3 7.9 slice-start.2
  114.4 5.8 slice-start.3
  116.7 3.5 copy-start.1
  135.0 2.4 copy-start.51
  136.7 2.0 copy-start.23
  136.8 2.1 copy-start.53
  138.2 2.3 copy-start.30
  139.7 5.7 copy-start.40
  140.5 3.1 copy-start.21
  140.6 3.1 copy-start.47
  140.6 3.1 copy-start.49
  142.2 12.3 %copy-start.11 = (f32[512,2,1,256]{3,0,1,2:T(8,128)}, f32[512,2,1,256]{3,0,1,2:T(8,128)S(1)}, u32[]{:S(2)}) copy-start(f32[512,2,1,256]{3,0,1,2:T(8,128)S(1)} %convolution_bitcast_fusion.2) | copy-start | bytes 3145732
  142.2 3.6 copy-start.7
  147.2 2.8 copy-start.37
  150.0 196.2 %reduce-scatter.5.cloned.1.call-start = ((), (), s32[]{:S(2)}) async-start(), calls=%async_computation.8 | async-start | bytes 7077888 | tf_op jit(solution)/shard_map/reduce_scatter | solution.py:341
  151.8 2.7 copy-start.13
  155.6 4.3 copy-start.22
  157.0 3.4 copy-start.44
  157.1 3.4 copy-start.45
  166.0 9.6 copy-start.2
  166.0 9.5 copy-start.52
  184.6 421.0 %all-reduce.12.cloned.1.call-start = ((), (), s32[]{:S(2)}) async-start(), calls=%async_computation.14 | async-start | bytes 16777216 | tf_op jit(solution)/shard_map/psum | solution.py:288
  210.5 11.4 %copy-start.61 = (bf16[2048,2048]{1,0:T(8,128)(2,1)S(1)}, bf16[2048,2048]{1,0:T(8,128)(2,1)}, u32[]{:S(2)}) copy-start(bf16[2048,2048]{1,0:T(8,128)(2,1)} %all-gather.20.cloned.1.call-done) | copy-start | bytes 25165828
  221.9 5.8 copy-start.3
  221.9 12.4 %slice-start = ((s8[8388608]{0:T(1024)(128)(4,1)}), s8[4194304]{0:T(1024)(128)(4,1)S(1)}, s32[]{:S(2)}) async-start(s8[8388608]{0:T(1024)(128)(4,1)} %bitcast.167), calls=%async_computation.15 | async-start | bytes 8388608
  227.7 6.7 copy-start.8
  227.7 6.7 slice-start.1
  249.6 9.4 copy-start.35
  249.6 9.4 copy-start.41
  249.6 506.8 %all-gather.24.cloned.1.call-start = ((), (), s32[]{:S(2)}) async-start(), calls=%async_computation.12 | async-start | bytes 10485760 | tf_op jit(solution)/shard_map/all_gather | solution.py:235
  261.7 10.1 copy-start.39
  261.7 644.1 %all-gather.26.cloned.1.call-start = ((), (), s32[]{:S(2)}) async-start(), calls=%async_computation.13 | async-start | bytes 10485760 | tf_op jit(solution)/shard_map/all_gather | solution.py:235
  274.6 704.0 %reduce-scatter.11.cloned.1.call-start = ((), (), s32[]{:S(2)}) async-start(), calls=%async_computation.11 | async-start | bytes 9437184 | tf_op jit(solution)/shard_map/reduce_scatter | solution.py:359
  274.6 13.7 %copy-start.9 = (bf16[1024,2048]{1,0:T(8,128)(2,1)S(1)}, bf16[1024,2048]{1,0:T(8,128)(2,1)}, u32[]{:S(2)}) copy-start(bf16[1024,2048]{1,0:T(8,128)(2,1)} %param.31) | copy-start | bytes 12582916
  274.6 13.7 %copy-start.64 = (f32[512,2048]{1,0:T(8,128)S(1)}, f32[512,2048]{1,0:T(8,128)}, u32[]{:S(2)}) copy-start(f32[512,2048]{1,0:T(8,128)} %fusion.98) | copy-start | bytes 12582916
  299.0 754.6 %reduce-scatter.9.cloned.1.call-start = ((), (), s32[]{:S(2)}) async-start(), calls=%async_computation.10 | async-start | bytes 9437184 | tf_op jit(solution)/shard_map/reduce_scatter | solution.py:353
  300.8 10.3 copy-start.4
  322.4 19.7 %copy-start.12 = (f32[512,2,1,256]{3,0,1,2:T(8,128)S(1)}, f32[512,2,1,256]{3,0,1,2:T(8,128)}, u32[]{:S(2)}) copy-start(f32[512,2,1,256]{3,0,1,2:T(8,128)} %copy-done.11) | copy-start | bytes 3145732
  322.4 19.7 %copy-start.14 = (f32[512,2,1,256]{3,0,1,2:T(8,128)S(1)}, f32[512,2,1,256]{3,0,1,2:T(8,128)}, u32[]{:S(2)}) copy-start(f32[512,2,1,256]{3,0,1,2:T(8,128)} %copy-done.13) | copy-start | bytes 3145732
  322.4 19.7 %copy-start.16 = (f32[512,2,1,256]{3,0,1,2:T(8,128)S(1)}, f32[512,2,1,256]{3,0,1,2:T(8,128)}, u32[]{:S(2)}) copy-start(f32[512,2,1,256]{3,0,1,2:T(8,128)} %copy-done.15) | copy-start | bytes 3145732
  342.1 263.6 %copy-start.58 = (f32[8,1,256]{2,1,0:T(1,128)S(1)}, f32[8,1,256]{2,1,0:T(1,128)}, u32[]{:S(2)}) copy-start(f32[8,1,256]{2,1,0:T(1,128)} %copy-done.57) | copy-start | bytes 24580
  605.6 9.7 copy-start.5
  605.6 9.8 copy-start.10
  605.6 9.8 copy-start.27
  605.6 9.8 copy-start.28
  645.8 410.6 %copy-start.60 = (f32[256]{0:T(256)}, f32[256]{0:T(256)S(1)}, u32[]{:S(2)}) copy-start(f32[256]{0:T(256)S(1)} %dynamic-slice_convert_fusion.1) | copy-start | bytes 3076
  913.0 68.3 %copy-start.26 = (bf16[512,2048]{1,0:T(8,128)(2,1)S(1)}, bf16[512,2048]{1,0:T(8,128)(2,1)}, u32[]{:S(2)}) copy-start(bf16[512,2048]{1,0:T(8,128)(2,1)} %get-tuple-element.150) | copy-start | bytes 6291460
  988.9 3.0 copy-start.29
  (19 other events, 29.7 us)
Sparse Core Ops, SparseCore 0:
  9.9 30.8 all-gather.17
  42.7 45.4 all-gather.15
  90.0 54.2 all-gather.19
  146.1 55.8 all-gather.21
  205.1 41.1 reduce-scatter.6
  249.5 61.7 reduce-scatter.4
  314.7 290.8 all-reduce.11
  607.8 148.5 all-gather.23
  758.0 147.7 all-gather.25
  909.1 69.4 reduce-scatter.10
  982.1 71.4 reduce-scatter.8
